TPU v7x, 256 devices: a whole 4x4x8 slice. The times are simulated.
256 devices in a mesh: shot: 8 (over y, z_lo), space: 32 (over x, z_hi, core).
Axes of the slice: x: 4, y: 4, z: 8 (z_hi: 4, z_lo: 2; z = z_hi * 2 + z_lo), core: 2. Of those that a mesh axis runs over, the one named last changes fastest.
Arguments:
- wave_prev: float32 [8, 512, 128, 128], P('shot', 'space'), may hold values from -6 to 6
- wave_now: float32 [8, 512, 128, 128], P('shot', 'space'), may hold values from -6 to 6
- velocity: float32 [512, 128, 128], P('space'), may hold values from 0.05 to 0.2
- probe_panel: float32 [4, 512, 128, 128], P(None, 'space', 'shot'), may hold values from -6 to 6
- source_depth: int32 [8], P('shot'), may hold values from 0 to 511
- source_column: int32 [8], P('shot'), may hold values from 0 to 16383
- source_strength: float32 [8], P('shot'), may hold values from 2 to 6
- receiver_wells: int32 [8, 512], P('shot'), may hold values from 0 to 16383
Outputs:
- hessian_action: float32 [4, 512, 128, 128], P(None, 'space', 'shot')
All inputs are finite; a program needn't handle non-finite values.
Results may differ from a plain program's by a relative error of at most 0.0003.
Values sent between devices are 32-bit elements; how exact they have to be, the bound alone decides.
No kernel may reach another device: no remote copies, remote signals or barrier semaphores. Data moves between devices by JAX's collectives and lax.ppermute only.
A program may use at most 128 MiB of HBM per device.

v0:
```python
import jax
import jax.numpy as jnp
from jax import lax
from jax.sharding import PartitionSpec as P

CENTER = -205.0 / 72.0
WEIGHTS = (8.0 / 5.0, -1.0 / 5.0, 8.0 / 315.0, -1.0 / 560.0)


def extended(block, sides, width):
    for axis, dim in sides:
        count = lax.axis_size(axis)
        forward = [(i, i + 1) for i in range(count - 1)]
        backward = [(target, source) for source, target in forward]
        low = lax.ppermute(
            lax.slice_in_dim(block, block.shape[dim] - width, None, axis=dim), axis, forward
        )
        high = lax.ppermute(lax.slice_in_dim(block, 0, width, axis=dim), axis, backward)
        block = jnp.concatenate([low, block, high], axis=dim)
    return block


def laplace(padded):
    count_rows = padded.shape[-3] - 8
    middle = padded[..., 4 : 4 + count_rows, :, :]
    count_x = middle.shape[-2]
    count_y = middle.shape[-1]
    lead_pads = [(0, 0)] * (middle.ndim - 2)
    wide_x = jnp.pad(middle, lead_pads + [(4, 4), (0, 0)])
    wide_y = jnp.pad(middle, lead_pads + [(0, 0), (4, 4)])
    stencil = 3.0 * CENTER * middle
    for offset in range(1, 5):
        weight = WEIGHTS[offset - 1]
        stencil = stencil + weight * (
            padded[..., 4 + offset : 4 + offset + count_rows, :, :]
            + padded[..., 4 - offset : 4 - offset + count_rows, :, :]
        )
        stencil = stencil + weight * (
            wide_x[..., 4 + offset : 4 + offset + count_x, :]
            + wide_x[..., 4 - offset : 4 - offset + count_x, :]
        )
        stencil = stencil + weight * (
            wide_y[..., 4 + offset : 4 + offset + count_y]
            + wide_y[..., 4 - offset : 4 - offset + count_y]
        )
    return stencil


def tally(wells, columns):
    return jnp.zeros((columns,), jnp.float32).at[wells].add(1.0)


def per_device(
    wave_prev,
    wave_now,
    velocity,
    probe_panel,
    source_depth,
    source_column,
    source_strength,
    receiver_wells,
):
    shot_count = wave_now.shape[0]
    count_z = wave_now.shape[1]
    width_x = wave_now.shape[2]
    width_y = wave_now.shape[3]
    probe_count = probe_panel.shape[0]
    columns = width_x * width_y
    probes = lax.all_gather(probe_panel, "shot", axis=2, tiled=True)
    first_row = lax.axis_index("space") * count_z
    column_ids = jnp.arange(columns, dtype=jnp.int32).reshape(width_x, width_y)
    now_wide = extended(wave_now, (("space", 1),), 4)
    born_zero = velocity * laplace(now_wide)
    depth_rows = first_row + jnp.arange(count_z, dtype=jnp.int32)
    hit_depth = depth_rows[None, :] == source_depth[:, None]
    hit_column = column_ids[None, :, :] == source_column[:, None, None]
    marks = (hit_depth[:, :, None, None] & hit_column[:, None, :, :]).astype(jnp.float32)
    upcoming = 2.0 * wave_now - wave_prev + born_zero + marks * source_strength[:, None, None, None]
    next_wide = extended(upcoming, (("space", 1),), 4)
    born_one = velocity * laplace(next_wide)
    first_field = probes[:, None] * born_zero[None]
    flat_first = first_field.reshape(probe_count * shot_count, count_z, width_x, width_y)
    first_wide = extended(flat_first, (("space", 1),), 4)
    first_wide = first_wide.reshape(probe_count, shot_count, count_z + 8, width_x, width_y)
    second_field = (
        2.0 * first_field + velocity * laplace(first_wide) + probes[:, None] * born_one[None]
    )
    counts = jax.vmap(lambda wells: tally(wells, columns))(receiver_wells)
    counts = counts.reshape(shot_count, width_x, width_y)[None, :, None]
    late_field = counts * second_field
    weighted = velocity * late_field
    flat_weighted = weighted.reshape(probe_count * shot_count, count_z, width_x, width_y)
    weighted_wide = extended(flat_weighted, (("space", 1),), 4)
    weighted_wide = weighted_wide.reshape(probe_count, shot_count, count_z + 8, width_x, width_y)
    early_field = counts * first_field + 2.0 * late_field + laplace(weighted_wide)
    local_sum = jnp.sum(born_zero[None] * early_field + born_one[None] * late_field, axis=1)
    summed = lax.psum(local_sum, "shot")
    share_rows = width_x // lax.axis_size("shot")
    summed = lax.dynamic_slice_in_dim(summed, lax.axis_index("shot") * share_rows, share_rows, 2)
    return summed / (shot_count * lax.axis_size("shot"))


def solution(mesh):
    return jax.shard_map(
        per_device,
        mesh=mesh,
        in_specs=(
            P("shot", "space", None, None),
            P("shot", "space", None, None),
            P("space", None, None),
            P(None, "space", "shot", None),
            P("shot"),
            P("shot"),
            P("shot"),
            P("shot", None),
        ),
        out_specs=P(None, "space", "shot", None),
        check_vma=False,
    )
```

profile of v0, /device:TPU:1, one launch (start us, length us, event | category | flops | bytes accessed | tf_op | source)
XLA Modules:
  0.0 496.8 jit_solution(8615643306405731458)
XLA Ops:
  6.5 0.0 all-gather.2.cloned.1.call-start
  6.5 0.7 all-gather.2.cloned.1.call-update
  7.3 0.0 all-reduce.10.cloned.1.call-start
  7.3 1.1 fusion.131
  8.4 5.1 %collective-permute-start = (f32[1,4,128,128]{3,2,1,0:T(8,128)S(1)}, f32[1,4,128,128]{3,2,1,0:T(8,128)S(1)}, u32[]{:S(2)}, u32[]{:S(2)}) collective-permute-start(f32[1,4,128,128]{3,2,1,0:T(8,128)S(1)} %get-tuple-element.15), channel_id=1, source_target_pairs={{1,0},{2,1},{3,2},{4,3},{5,4},{6,5},{7,6},{8,7},{9,8},{10,9},{11,1... | collective-permute-start | bytes 786440 | tf_op jit(solution)/shard_map/ppermute | solution.py:18
  13.5 3.1 collective-permute-start.1
  17.9 0.0 copy-start.7
  18.7 0.7 fusion.125
  19.4 0.6 collective-permute-done.1
  20.0 1.5 constant_dynamic-update-slice_fusion.1
  21.5 0.1 collective-permute-done
  21.5 0.0 copy-done.5
  21.5 0.0 copy-done.4
  21.6 0.0 copy-done.7
  21.6 3.7 select_add_fusion
  25.3 80.6 %all-gather.2.cloned.1.call-done = f32[4,16,128,128]{3,2,1,0:T(8,128)} async-done(((f32[4,16,16,128]{3,2,1,0:T(8,128)}), f32[4,16,128,128]{3,2,1,0:T(8,128)}) %all-gather.2.cloned.1.call-update) | async-done | bytes 4194320 | tf_op jit(solution)/shard_map/all_gather | solution.py:69
  105.9 2.6 broadcast_multiply_fusion
  108.5 1.9 copy-done.3
  110.4 1.6 fusion.129
  112.0 5.2 %collective-permute-start.2 = (f32[4,4,128,128]{3,2,1,0:T(8,128)}, f32[4,4,128,128]{3,2,1,0:T(8,128)}, u32[]{:S(2)}, u32[]{:S(2)}) collective-permute-start(f32[4,4,128,128]{3,2,1,0:T(8,128)} %get-tuple-element.11), channel_id=1, source_target_pairs={{0,1},{1,2},{2,3},{3,4},{4,5},{5,6},{6,7},{7,8},{8,9},{9,10},{10,1... | collective-permute-start | bytes 3145736 | tf_op jit(solution)/shard_map/ppermute | solution.py:15
  117.2 1.9 collective-permute-start.3
  119.2 0.0 copy-done.6
  119.2 0.8 fusion.130
  120.0 1.9 collective-permute-start.4
  121.9 4.5 collective-permute-start.5
  126.5 3.3 scatter_custom_fusion
  129.8 21.5 %collective-permute-done.4 = f32[1,4,128,128]{3,2,1,0:T(8,128)S(1)} collective-permute-done((f32[1,4,128,128]{3,2,1,0:T(8,128)}, f32[1,4,128,128]{3,2,1,0:T(8,128)S(1)}, u32[]{:S(2)}, u32[]{:S(2)}) %collective-permute-start.4) | collective-permute-done | bytes 262176 | tf_op jit(solution)/shard_map/ppermute | solution.py:18
  151.3 0.0 collective-permute-done.5
  151.3 15.7 %fusion.66 = f32[16,128,128]{2,1,0:T(8,128)S(1)} fusion(f32[1,16,128,128]{3,2,1,0:T(8,128)} %get-tuple-element.7, f32[1,4,128,128]{3,2,1,0:T(8,128)} %collective-permute-done.5, f32[1,4,128,128]{3,2,1,0:T(8,128)S(1)} %collective-permute-done.4, f32[16,128,128]{2,1,0:T(8,128)S(1)} %copy-done.4), kind=kLoop, calls=%fused_computation.126 | loop fusion | flops 12058624 | bytes 3670016 | tf_op jit(solution)/shard_map/mul | solution.py:86
  167.0 0.0 collective-permute-done.2
  167.0 0.0 collective-permute-done.3
  167.0 3.2 maximum_bitcast_fusion
  170.3 2.6 copy-done.1
  172.9 2.2 slice.454
  175.1 42.2 %multiply_bitcast_fusion = (f32[4,16,128,128]{3,2,1,0:T(8,128)}, f32[4,1,16,128,128]{4,3,2,0,1:T(8,128)}) fusion(f32[16,128,128]{2,1,0:T(8,128)S(1)} %copy-done.4, f32[4,16,128,128]{3,2,1,0:T(8,128)} %all-gather.2.cloned.1.call-done, f32[16,128,128]{2,1,0:T(8,128)S(1)} %fusion.66, f32[4,1,24,128,128]{4,3,2,0,1:T(8,128)} %copy-done.1, ...), kind=kLoop, calls=%fused_computation.99 | loop fusion | flops 47185920 | bytes 53542912 | tf_op jit(solution)/shard_map/reshape | solution.py:92
  217.4 1.8 fusion.128
  219.2 2.1 collective-permute-start.6
  221.3 2.6 collective-permute-start.7
  223.9 13.0 %collective-permute-done.6 = f32[4,4,128,128]{3,2,1,0:T(8,128)S(1)} collective-permute-done((f32[4,4,128,128]{3,2,1,0:T(8,128)S(1)}, f32[4,4,128,128]{3,2,1,0:T(8,128)S(1)}, u32[]{:S(2)}, u32[]{:S(2)}) %collective-permute-start.6) | collective-permute-done | bytes 1048608 | tf_op jit(solution)/shard_map/ppermute | solution.py:15
  237.0 10.9 %collective-permute-done.7 = f32[4,4,128,128]{3,2,1,0:T(8,128)S(1)} collective-permute-done((f32[4,4,128,128]{3,2,1,0:T(8,128)S(1)}, f32[4,4,128,128]{3,2,1,0:T(8,128)S(1)}, u32[]{:S(2)}, u32[]{:S(2)}) %collective-permute-start.7) | collective-permute-done | bytes 1048608 | tf_op jit(solution)/shard_map/ppermute | solution.py:18
  247.8 0.0 copy-done.2
  247.8 0.8 maximum_bitcast_fusion.1
  248.6 2.5 slice.479
  251.1 1.6 copy-done
  252.7 46.0 %fusion.55 = f32[4,16,128,128]{3,2,1,0:T(8,128)} fusion(f32[4,1,16,128,128]{4,3,2,0,1:T(8,128)} %get-tuple-element.6, f32[4,1,16,128,128]{4,3,2,0,1:T(8,128)} %slice.479, f32[4,1,24,128,128]{4,3,2,0,1:T(8,128)} %copy-done, f32[16,128,128]{2,1,0:T(8,128)S(1)} %fusion.66, f32[128,128]{1,0:T(8,128)S(1)} %bitcast.47, f32[16,128,128]{2,1,0:T(8,128)S(1)} %bitcast.45, ...), kind=kLoop, calls=%fused_computation.102 | loop fusion | flops 47185920 | bytes 53542912 | tf_op jit(solution)/shard_map/reduce_sum | solution.py:96
  298.8 0.0 all-reduce.10.cloned.1.call-update
  298.8 189.2 %all-reduce.10.cloned.1.call-done = f32[4,16,128,128]{3,2,1,0:T(8,128)} async-done(((f32[4,16,128,128]{3,2,1,0:T(8,128)}), f32[4,16,128,128]{3,2,1,0:T(8,128)}) %all-reduce.10.cloned.1.call-update) | async-done | bytes 4194320 | tf_op jit(solution)/shard_map/psum | solution.py:97
  488.0 1.9 dynamic-slice_multiply_fusion
  (14 shorter events, 0.1 us)
Async XLA Ops:
  6.5 15.0 %copy-start.5 = (f32[1,16,128,128]{3,2,1,0:T(8,128)S(1)}, f32[1,16,128,128]{3,2,1,0:T(8,128)}, u32[]{:S(2)}) copy-start(f32[1,16,128,128]{3,2,1,0:T(8,128)} %param.9) | copy-start | bytes 3145732
  6.5 15.0 %copy-start.4 = (f32[16,128,128]{2,1,0:T(8,128)S(1)}, f32[16,128,128]{2,1,0:T(8,128)}, u32[]{:S(2)}) copy-start(f32[16,128,128]{2,1,0:T(8,128)} %param.10) | copy-start | bytes 3145732
  6.5 99.3 %all-gather.2.cloned.1.call-start = ((), (), s32[]{:S(2)}) async-start(), calls=%async_computation | async-start | bytes 4718592 | tf_op jit(solution)/shard_map/all_gather | solution.py:69
  7.3 480.8 %all-reduce.10.cloned.1.call-start = ((), (), s32[]{:S(2)}) async-start(), calls=%async_computation.1 | async-start | bytes 8388608 | tf_op jit(solution)/shard_map/psum | solution.py:97
  8.4 13.1 %collective-permute-start = (f32[1,4,128,128]{3,2,1,0:T(8,128)S(1)}, f32[1,4,128,128]{3,2,1,0:T(8,128)S(1)}, u32[]{:S(2)}, u32[]{:S(2)}) collective-permute-start(f32[1,4,128,128]{3,2,1,0:T(8,128)S(1)} %get-tuple-element.15), channel_id=1, source_target_pairs={{1,0},{2,1},{3,2},{4,3},{5,4},{6,5},{7,6},{8,7},{9,8},{10,9},{11,1... | collective-permute-start | bytes 786440 | tf_op jit(solution)/shard_map/ppermute | solution.py:18
  13.5 6.4 %collective-permute-start.1 = (f32[1,4,128,128]{3,2,1,0:T(8,128)S(1)}, f32[1,4,128,128]{3,2,1,0:T(8,128)S(1)}, u32[]{:S(2)}, u32[]{:S(2)}) collective-permute-start(f32[1,4,128,128]{3,2,1,0:T(8,128)S(1)} %get-tuple-element.16), channel_id=1, source_target_pairs={{0,1},{1,2},{2,3},{3,4},{4,5},{5,6},{6,7},{7,8},{8,9},{9,10},{10,1... | collective-permute-start | bytes 786440 | tf_op jit(solution)/shard_map/ppermute | solution.py:15
  17.9 3.7 copy-start.7
  108.5 1.9 copy-start.3
  110.4 8.7 %copy-start.6 = (f32[1,16,128,128]{3,2,1,0:T(8,128)S(1)}, f32[1,16,128,128]{3,2,1,0:T(8,128)}, u32[]{:S(2)}) copy-start(f32[1,16,128,128]{3,2,1,0:T(8,128)} %get-tuple-element.7) | copy-start | bytes 3145732
  112.0 55.0 %collective-permute-start.2 = (f32[4,4,128,128]{3,2,1,0:T(8,128)}, f32[4,4,128,128]{3,2,1,0:T(8,128)}, u32[]{:S(2)}, u32[]{:S(2)}) collective-permute-start(f32[4,4,128,128]{3,2,1,0:T(8,128)} %get-tuple-element.11), channel_id=1, source_target_pairs={{0,1},{1,2},{2,3},{3,4},{4,5},{5,6},{6,7},{7,8},{8,9},{9,10},{10,1... | collective-permute-start | bytes 3145736 | tf_op jit(solution)/shard_map/ppermute | solution.py:15
  117.2 49.8 %collective-permute-start.3 = (f32[4,4,128,128]{3,2,1,0:T(8,128)}, f32[4,4,128,128]{3,2,1,0:T(8,128)}, u32[]{:S(2)}, u32[]{:S(2)}) collective-permute-start(f32[4,4,128,128]{3,2,1,0:T(8,128)} %get-tuple-element.12), channel_id=1, source_target_pairs={{1,0},{2,1},{3,2},{4,3},{5,4},{6,5},{7,6},{8,7},{9,8},{10,9},{11,1... | collective-permute-start | bytes 3145736 | tf_op jit(solution)/shard_map/ppermute | solution.py:18
  120.0 31.3 %collective-permute-start.4 = (f32[1,4,128,128]{3,2,1,0:T(8,128)}, f32[1,4,128,128]{3,2,1,0:T(8,128)S(1)}, u32[]{:S(2)}, u32[]{:S(2)}) collective-permute-start(f32[1,4,128,128]{3,2,1,0:T(8,128)} %get-tuple-element.13), channel_id=1, source_target_pairs={{1,0},{2,1},{3,2},{4,3},{5,4},{6,5},{7,6},{8,7},{9,8},{10,9},{11,1... | collective-permute-start | bytes 786440 | tf_op jit(solution)/shard_map/ppermute | solution.py:18
  121.9 29.4 %collective-permute-start.5 = (f32[1,4,128,128]{3,2,1,0:T(8,128)}, f32[1,4,128,128]{3,2,1,0:T(8,128)}, u32[]{:S(2)}, u32[]{:S(2)}) collective-permute-start(f32[1,4,128,128]{3,2,1,0:T(8,128)} %get-tuple-element.14), channel_id=1, source_target_pairs={{0,1},{1,2},{2,3},{3,4},{4,5},{5,6},{6,7},{7,8},{8,9},{9,10},{10,1... | collective-permute-start | bytes 786440 | tf_op jit(solution)/shard_map/ppermute | solution.py:15
  170.3 2.7 copy-start.1
  217.4 30.5 %copy-start.2 = (f32[4,16,128,128]{3,2,1,0:T(8,128)S(1)}, f32[4,16,128,128]{3,2,1,0:T(8,128)}, u32[]{:S(2)}) copy-start(f32[4,16,128,128]{3,2,1,0:T(8,128)} %get-tuple-element.5) | copy-start | bytes 12582916
  219.2 17.7 %collective-permute-start.6 = (f32[4,4,128,128]{3,2,1,0:T(8,128)S(1)}, f32[4,4,128,128]{3,2,1,0:T(8,128)S(1)}, u32[]{:S(2)}, u32[]{:S(2)}) collective-permute-start(f32[4,4,128,128]{3,2,1,0:T(8,128)S(1)} %get-tuple-element.9), channel_id=1, source_target_pairs={{0,1},{1,2},{2,3},{3,4},{4,5},{5,6},{6,7},{7,8},{8,9},{9,10},{10,1... | collective-permute-start | bytes 3145736 | tf_op jit(solution)/shard_map/ppermute | solution.py:15
  221.3 26.5 %collective-permute-start.7 = (f32[4,4,128,128]{3,2,1,0:T(8,128)S(1)}, f32[4,4,128,128]{3,2,1,0:T(8,128)S(1)}, u32[]{:S(2)}, u32[]{:S(2)}) collective-permute-start(f32[4,4,128,128]{3,2,1,0:T(8,128)S(1)} %get-tuple-element.10), channel_id=1, source_target_pairs={{1,0},{2,1},{3,2},{4,3},{5,4},{6,5},{7,6},{8,7},{9,8},{10,9},{11,1... | collective-permute-start | bytes 3145736 | tf_op jit(solution)/shard_map/ppermute | solution.py:18
  248.6 4.1 copy-start
Sparse Core Ops, SparseCore 0:
  9.1 96.7 all-gather.1
  298.9 189.0 all-reduce.9
where the time goes:
time: 497 us
  waiting for transfers between devices  317 us (64%)
  other arithmetic  120 us (24%)
  starting transfers between devices  26.5 us (5%)
  local copies, waits for them, and re-layouts  17.7 us (4%)
  between operations  15.7 us (3%)
    psum x1, waiting for transfers between devices, per_device(): summed = lax.psum(local_sum, 'shot')  189 us
    all_gather x1, waiting for transfers between devices, per_device(): probes = lax.all_gather(probe_panel, 'shot', axis=2, tiled=True)  80.6 us
    reduce_sum x1, other arithmetic, per_device(): jnp.sum(born_zero[None] * early_field + born_one[None] * late_field, axis=1)  46 us
    reshape x1, other arithmetic, per_device(): weighted.reshape(probe_count * shot_count, count_z, width_x, width_y)  42.2 us
    ppermute x4, waiting for transfers between devices, extended(): lax.ppermute(lax.slice_in_dim(block, 0, width, axis=dim), axis, backward)  32.5 us
    mul x1, other arithmetic, per_device(): probes[:, None] * born_one[None]  15.7 us
    ppermute x4, starting transfers between devices, extended(): lax.ppermute(lax.slice_in_dim(block, block.shape[dim] - width, None, axis...  14.9 us
    ppermute x4, waiting for transfers between devices, extended(): lax.ppermute(lax.slice_in_dim(block, block.shape[dim] - width, None, axis...  13.6 us
  transfers between devices with their start and end apart: 10, of which 6 were waited for; matrix products, arithmetic and copies ran while one was open for 5% of the time, Pallas kernels for 0%

commit v1 on v0

--- a/solution.py
+++ b/solution.py
@@ -1,3 +1,4 @@
+import functools
 import jax
 import jax.numpy as jnp
 from jax import lax
@@ -5,6 +6,13 @@
 
 CENTER = -205.0 / 72.0
 WEIGHTS = (8.0 / 5.0, -1.0 / 5.0, 8.0 / 315.0, -1.0 / 560.0)
+
+
+def form_types(payload, axis_name):
+    return jnp.sum(lax.all_gather(payload, axis_name), axis=0)
+
+
+post_types = functools.partial(form_types, axis_name="shot")
 
 
 def extended(block, sides, width):
@@ -94,7 +102,7 @@
     weighted_wide = weighted_wide.reshape(probe_count, shot_count, count_z + 8, width_x, width_y)
     early_field = counts * first_field + 2.0 * late_field + laplace(weighted_wide)
     local_sum = jnp.sum(born_zero[None] * early_field + born_one[None] * late_field, axis=1)
-    summed = lax.psum(local_sum, "shot")
+    summed = post_types(local_sum)
     share_rows = width_x // lax.axis_size("shot")
     summed = lax.dynamic_slice_in_dim(summed, lax.axis_index("shot") * share_rows, share_rows, 2)
     return summed / (shot_count * lax.axis_size("shot"))

time: 497 us -> 960 us (1.93)
  waiting for transfers between devices: 317 us -> 772 us
    all_gather x0 -> x1, waiting for transfers between devices: none -> 644 us  [form_types(): return jnp.sum(lax.all_gather(payload, axis_name), axis=0)]
    psum x1 -> x0, waiting for transfers between devices: 189 us -> none  [per_device(): summed = lax.psum(local_sum, 'shot')]
    add x0 -> x1, other arithmetic: none -> 43 us  [per_device(): born_zero[None] * early_field + born_one[None] * late_field]
    reduce_sum x1, other arithmetic: 46 us -> 12.2 us  [form_types(): return jnp.sum(lax.all_gather(payload, axis_name), axis=0)]
  transfers between devices with their start and end apart: 10 -> 10, of which waited for: 6 -> 6; matrix products, arithmetic and copies ran while one was open for 5% -> 3% of each run, Pallas kernels for 0% -> 0%
where the time goes in v1:
time: 960 us
  waiting for transfers between devices  772 us (80%)
  other arithmetic  128 us (13%)
  starting transfers between devices  26.5 us (3%)
  local copies, waits for them, and re-layouts  17.6 us (2%)
  between operations  15.7 us (2%)
    all_gather x1, waiting for transfers between devices, form_types(): return jnp.sum(lax.all_gather(payload, axis_name), axis=0)  644 us
    all_gather x1, waiting for transfers between devices, per_device(): probes = lax.all_gather(probe_panel, 'shot', axis=2, tiled=True)  80.6 us
    add x1, other arithmetic, per_device(): born_zero[None] * early_field + born_one[None] * late_field  43 us
    reshape x1, other arithmetic, per_device(): weighted.reshape(probe_count * shot_count, count_z, width_x, width_y)  42.2 us
    ppermute x4, waiting for transfers between devices, extended(): lax.ppermute(lax.slice_in_dim(block, 0, width, axis=dim), axis, backward)  32.5 us
  transfers between devices with their start and end apart: 10, of which 6 were waited for; matrix products, arithmetic and copies ran while one was open for 3% of the time, Pallas kernels for 0%

profile of v1, /device:TPU:1, one launch (start us, length us, event | category | flops | bytes accessed | tf_op | source)
XLA Modules:
  0.0 959.8 jit_solution(5243197905707910539)
XLA Ops:
  6.5 0.0 all-gather.4.cloned.1.call-start
  6.5 0.7 all-gather.4.cloned.1.call-update
  7.3 0.0 all-gather.6.cloned.1.call-start
  7.3 1.1 fusion.129
  8.4 5.1 collective-permute-start
  13.5 3.1 collective-permute-start.1
  17.9 0.0 copy-start.7
  18.7 0.7 fusion.124
  19.4 0.6 collective-permute-done.1
  20.0 1.5 constant_dynamic-update-slice_fusion.1
  21.5 0.1 collective-permute-done
  21.5 0.0 copy-done.5
  21.5 0.0 copy-done.4
  21.6 3.7 select_add_fusion
  25.3 80.6 %all-gather.4.cloned.1.call-done = f32[4,16,128,128]{3,2,1,0:T(8,128)} async-done(((f32[4,16,16,128]{3,2,1,0:T(8,128)}), f32[4,16,128,128]{3,2,1,0:T(8,128)}) %all-gather.4.cloned.1.call-update) | async-done | bytes 4194320 | tf_op jit(solution)/shard_map/all_gather | solution.py:77
  105.9 2.6 broadcast_multiply_fusion
  108.5 1.9 copy-done.3
  110.4 1.6 fusion.127
  112.0 5.2 collective-permute-start.2
  117.2 1.9 collective-permute-start.3
  119.2 0.0 copy-done.6
  119.2 0.8 fusion.128
  120.0 1.9 collective-permute-start.4
  121.9 4.5 collective-permute-start.5
  126.5 3.3 scatter_custom_fusion
  129.8 21.5 %collective-permute-done.4 = f32[1,4,128,128]{3,2,1,0:T(8,128)S(1)} collective-permute-done((f32[1,4,128,128]{3,2,1,0:T(8,128)}, f32[1,4,128,128]{3,2,1,0:T(8,128)S(1)}, u32[]{:S(2)}, u32[]{:S(2)}) %collective-permute-start.4) | collective-permute-done | bytes 262176 | tf_op jit(solution)/shard_map/ppermute | solution.py:26
  151.3 0.0 collective-permute-done.5
  151.3 15.7 %fusion.65 = f32[16,128,128]{2,1,0:T(8,128)S(1)} fusion(f32[1,16,128,128]{3,2,1,0:T(8,128)} %get-tuple-element.7, f32[1,4,128,128]{3,2,1,0:T(8,128)} %collective-permute-done.5, f32[1,4,128,128]{3,2,1,0:T(8,128)S(1)} %collective-permute-done.4, f32[16,128,128]{2,1,0:T(8,128)S(1)} %copy-done.4), kind=kLoop, calls=%fused_computation.128 | loop fusion | flops 12058624 | bytes 3670016 | tf_op jit(solution)/shard_map/mul | solution.py:94
  167.0 0.0 collective-permute-done.2
  167.0 0.0 collective-permute-done.3
  167.0 3.2 maximum_bitcast_fusion
  170.3 2.6 copy-done.1
  172.9 2.2 slice.454
  175.1 42.2 %fusion.53 = (f32[4,16,128,128]{3,2,1,0:T(8,128)}, f32[4,1,16,128,128]{4,3,2,1,0:T(8,128)}) fusion(f32[16,128,128]{2,1,0:T(8,128)S(1)} %copy-done.4, f32[4,16,128,128]{3,2,1,0:T(8,128)} %all-gather.4.cloned.1.call-done, f32[16,128,128]{2,1,0:T(8,128)S(1)} %fusion.65, f32[4,1,24,128,128]{4,3,2,0,1:T(8,128)} %copy-done.1, f32[4,1,16,128,128]{4,3,2,0,1:T(8,128)} %slice.454, ...), kind=kLoop, calls=%fused_computation.99 | loop fusion | flops 47185920 | bytes 53542912 | tf_op jit(solution)/shard_map/reshape | solution.py:100
  217.4 1.8 fusion.126
  219.2 2.1 collective-permute-start.6
  221.3 2.6 collective-permute-start.7
  223.9 13.0 %collective-permute-done.6 = f32[4,4,128,128]{3,2,1,0:T(8,128)S(1)} collective-permute-done((f32[4,4,128,128]{3,2,1,0:T(8,128)S(1)}, f32[4,4,128,128]{3,2,1,0:T(8,128)S(1)}, u32[]{:S(2)}, u32[]{:S(2)}) %collective-permute-start.6) | collective-permute-done | bytes 1048608 | tf_op jit(solution)/shard_map/ppermute | solution.py:23
  237.0 10.9 %collective-permute-done.7 = f32[4,4,128,128]{3,2,1,0:T(8,128)S(1)} collective-permute-done((f32[4,4,128,128]{3,2,1,0:T(8,128)S(1)}, f32[4,4,128,128]{3,2,1,0:T(8,128)S(1)}, u32[]{:S(2)}, u32[]{:S(2)}) %collective-permute-start.7) | collective-permute-done | bytes 1048608 | tf_op jit(solution)/shard_map/ppermute | solution.py:26
  247.8 0.0 copy-done.2
  247.8 0.8 maximum_bitcast_fusion.1
  248.6 2.4 slice.479
  251.0 1.5 copy-done
  252.5 43.0 %bitcast_add_fusion = f32[4,1,16,128,128]{4,3,2,1,0:T(8,128)} fusion(f32[4,1,16,128,128]{4,3,2,1,0:T(8,128)} %get-tuple-element.6, f32[4,1,16,128,128]{4,3,2,0,1:T(8,128)} %slice.479, f32[4,1,24,128,128]{4,3,2,0,1:T(8,128)} %copy-done, f32[16,128,128]{2,1,0:T(8,128)S(1)} %fusion.65, f32[128,128]{1,0:T(8,128)S(1)} %bitcast.64, ...), kind=kLoop, calls=%fused_computation.97 | loop fusion | flops 47185920 | bytes 53542912 | tf_op jit(solution)/shard_map/add | solution.py:104
  295.6 0.0 all-gather.6.cloned.1.call-update
  295.6 644.3 %all-gather.6.cloned.1.call-done = f32[32,1,16,128,128]{4,3,2,1,0:T(8,128)} async-done(((f32[4,1,16,128,128]{4,3,2,1,0:T(8,128)}), f32[32,1,16,128,128]{4,3,2,1,0:T(8,128)}) %all-gather.6.cloned.1.call-update) | async-done | bytes 33554448 | tf_op jit(solution)/shard_map/all_gather | solution.py:12
  939.9 12.2 %bitcast_reduce_fusion = f32[4,16,128,128]{3,2,1,0:T(8,128)S(1)} fusion(f32[8,4,16,128,128]{4,3,2,1,0:T(8,128)} %bitcast.59), kind=kLoop, calls=%fused_computation.1 | loop fusion | flops 7340032 | bytes 37748736 | tf_op jit(solution)/shard_map/reduce_sum | solution.py:12
  952.1 0.9 dynamic-slice_multiply_fusion
  (15 shorter events, 0.1 us)
Async XLA Ops:
  6.5 15.0 %copy-start.5 = (f32[1,16,128,128]{3,2,1,0:T(8,128)S(1)}, f32[1,16,128,128]{3,2,1,0:T(8,128)}, u32[]{:S(2)}) copy-start(f32[1,16,128,128]{3,2,1,0:T(8,128)} %param.9) | copy-start | bytes 3145732
  6.5 15.0 %copy-start.4 = (f32[16,128,128]{2,1,0:T(8,128)S(1)}, f32[16,128,128]{2,1,0:T(8,128)}, u32[]{:S(2)}) copy-start(f32[16,128,128]{2,1,0:T(8,128)} %param.10) | copy-start | bytes 3145732
  6.5 99.3 %all-gather.4.cloned.1.call-start = ((), (), s32[]{:S(2)}) async-start(), calls=%async_computation | async-start | bytes 4718592 | tf_op jit(solution)/shard_map/all_gather | solution.py:77
  7.3 932.7 %all-gather.6.cloned.1.call-start = ((), (), s32[]{:S(2)}) async-start(), calls=%async_computation.1 | async-start | bytes 37748736 | tf_op jit(solution)/shard_map/all_gather | solution.py:12
  8.4 13.1 %collective-permute-start = (f32[1,4,128,128]{3,2,1,0:T(8,128)S(1)}, f32[1,4,128,128]{3,2,1,0:T(8,128)S(1)}, u32[]{:S(2)}, u32[]{:S(2)}) collective-permute-start(f32[1,4,128,128]{3,2,1,0:T(8,128)S(1)} %get-tuple-element.15), channel_id=1, source_target_pairs={{1,0},{2,1},{3,2},{4,3},{5,4},{6,5},{7,6},{8,7},{9,8},{10,9},{11,1... | collective-permute-start | bytes 786440 | tf_op jit(solution)/shard_map/ppermute | solution.py:26
  13.5 6.4 collective-permute-start.1
  17.9 3.7 copy-start.7
  108.5 1.9 copy-start.3
  110.4 8.7 copy-start.6
  112.0 55.0 %collective-permute-start.2 = (f32[4,4,128,128]{3,2,1,0:T(8,128)}, f32[4,4,128,128]{3,2,1,0:T(8,128)}, u32[]{:S(2)}, u32[]{:S(2)}) collective-permute-start(f32[4,4,128,128]{3,2,1,0:T(8,128)} %get-tuple-element.11), channel_id=1, source_target_pairs={{0,1},{1,2},{2,3},{3,4},{4,5},{5,6},{6,7},{7,8},{8,9},{9,10},{10,1... | collective-permute-start | bytes 3145736 | tf_op jit(solution)/shard_map/ppermute | solution.py:23
  117.2 49.8 %collective-permute-start.3 = (f32[4,4,128,128]{3,2,1,0:T(8,128)}, f32[4,4,128,128]{3,2,1,0:T(8,128)}, u32[]{:S(2)}, u32[]{:S(2)}) collective-permute-start(f32[4,4,128,128]{3,2,1,0:T(8,128)} %get-tuple-element.12), channel_id=1, source_target_pairs={{1,0},{2,1},{3,2},{4,3},{5,4},{6,5},{7,6},{8,7},{9,8},{10,9},{11,1... | collective-permute-start | bytes 3145736 | tf_op jit(solution)/shard_map/ppermute | solution.py:26
  120.0 31.3 %collective-permute-start.4 = (f32[1,4,128,128]{3,2,1,0:T(8,128)}, f32[1,4,128,128]{3,2,1,0:T(8,128)S(1)}, u32[]{:S(2)}, u32[]{:S(2)}) collective-permute-start(f32[1,4,128,128]{3,2,1,0:T(8,128)} %get-tuple-element.13), channel_id=1, source_target_pairs={{1,0},{2,1},{3,2},{4,3},{5,4},{6,5},{7,6},{8,7},{9,8},{10,9},{11,1... | collective-permute-start | bytes 786440 | tf_op jit(solution)/shard_map/ppermute | solution.py:26
  121.9 29.4 %collective-permute-start.5 = (f32[1,4,128,128]{3,2,1,0:T(8,128)}, f32[1,4,128,128]{3,2,1,0:T(8,128)}, u32[]{:S(2)}, u32[]{:S(2)}) collective-permute-start(f32[1,4,128,128]{3,2,1,0:T(8,128)} %get-tuple-element.14), channel_id=1, source_target_pairs={{0,1},{1,2},{2,3},{3,4},{4,5},{5,6},{6,7},{7,8},{8,9},{9,10},{10,1... | collective-permute-start | bytes 786440 | tf_op jit(solution)/shard_map/ppermute | solution.py:23
  170.3 2.7 copy-start.1
  217.4 30.5 %copy-start.2 = (f32[4,16,128,128]{3,2,1,0:T(8,128)S(1)}, f32[4,16,128,128]{3,2,1,0:T(8,128)}, u32[]{:S(2)}) copy-start(f32[4,16,128,128]{3,2,1,0:T(8,128)} %get-tuple-element.5) | copy-start | bytes 12582916
  219.2 17.7 %collective-permute-start.6 = (f32[4,4,128,128]{3,2,1,0:T(8,128)S(1)}, f32[4,4,128,128]{3,2,1,0:T(8,128)S(1)}, u32[]{:S(2)}, u32[]{:S(2)}) collective-permute-start(f32[4,4,128,128]{3,2,1,0:T(8,128)S(1)} %get-tuple-element.9), channel_id=1, source_target_pairs={{0,1},{1,2},{2,3},{3,4},{4,5},{5,6},{6,7},{7,8},{8,9},{9,10},{10,1... | collective-permute-start | bytes 3145736 | tf_op jit(solution)/shard_map/ppermute | solution.py:23
  221.3 26.5 %collective-permute-start.7 = (f32[4,4,128,128]{3,2,1,0:T(8,128)S(1)}, f32[4,4,128,128]{3,2,1,0:T(8,128)S(1)}, u32[]{:S(2)}, u32[]{:S(2)}) collective-permute-start(f32[4,4,128,128]{3,2,1,0:T(8,128)S(1)} %get-tuple-element.10), channel_id=1, source_target_pairs={{1,0},{2,1},{3,2},{4,3},{5,4},{6,5},{7,6},{8,7},{9,8},{10,9},{11,1... | collective-permute-start | bytes 3145736 | tf_op jit(solution)/shard_map/ppermute | solution.py:26
  248.6 3.9 copy-start
Sparse Core Ops, SparseCore 0:
  9.1 96.7 all-gather.3
  295.7 644.1 all-gather.5
